TPU v7x, 512 devices: a whole 4x8x8 slice. The times are simulated.
512 devices in a mesh: dp: 64 (over x, y, core), tensor: 8 (over z).
Axes of the slice: x: 4, y: 8, z: 8, core: 2. Of those that a mesh axis runs over, the one named last changes fastest.
Arguments:
- features: bfloat16 [65536, 4096], P(('dp', 'tensor')), may hold values from -20 to 20
- key_grads: bfloat16 [65536, 1024], P('dp', 'tensor'), may hold values from -20 to 20
- error_in: bfloat16 [64, 4096, 1024], P('dp', None, 'tensor'), may hold values from -24 to 24
- selected: int32 [64, 8, 128], P('dp', 'tensor'), may hold values from 0 to 4095, as said below
- bin_edges: int32 [17], replicated, may hold values from 0 to 4096, as said below
- threshold: int32 [1], replicated, may hold values from 1 to 15
- moment: float32 [4096, 1024], P('dp', 'tensor'), may hold values from -2 to 2
- second: float32 [4096, 1024], P('dp', 'tensor'), may hold values from 0.05 to 2
- master: float32 [4096, 1024], P('dp', 'tensor'), may hold values from -0.0625 to 0.0625
Outputs:
- keys: bfloat16 [65536, 1024], P('dp', 'tensor')
- error_out: bfloat16 [64, 4096, 1024], P('dp', None, 'tensor')
- moment_new: float32 [4096, 1024], P('dp', 'tensor')
- second_new: float32 [4096, 1024], P('dp', 'tensor')
- master_new: float32 [4096, 1024], P('dp', 'tensor')
Inputs may be any that keep to these rules, and one draw needn't show every extreme that they name: Each device's 128 rows are distinct; the rows o * 64 to (o + 1) * 64 - 1 form owner o's region, and one device's row of selected names at most 6 rows of one region; there is one region, the same for every row of selected, that receives exactly 6 blocks from each row; every other region receives at most 6 from a row. bin_edges[0] = 0, bin_edges[16] = 4096, strictly increasing.
All inputs are finite; a program needn't handle non-finite values.
Results may differ from a plain program's by a relative error of at most 0.001.
The roundings to bfloat16 on the way count: a program that leaves them out, or rounds other values in their place, can miss the bound.
Values may be sent and summed in bfloat16 or wider, within the bound.
A program may use at most 64 MiB of HBM per device.

v0:
```python
import math
import jax
import jax.numpy as jnp
from jax import lax
from jax.sharding import PartitionSpec as P

CAP = 6
beta_first = 0.9
beta_second = 0.95
learn_rate = 0.001
decay_rate = 0.1
epsilon = 1e-06
adam_epsilon = 1e-08
step_count = 10.0


def copy_for_each(value, axis):
    devices = lax.axis_size(axis)
    return lax.all_to_all(
        jnp.broadcast_to(value[None], (devices, *value.shape)), axis, 0, 0, tiled=True
    )


def over_copies(value, axis):
    everything = copy_for_each(value, axis)
    return jnp.sum(everything, axis=0)


def in_one_piece(arrays, axis, split_dim, concat_dim, along):
    widths = [math.prod(a.shape[along:]) for a in arrays]
    both = jnp.concatenate(
        [a.reshape(*a.shape[:along], w) for a, w in zip(arrays, widths)], axis=along
    )
    filled = lax.all_to_all(both, axis, split_axis=split_dim, concat_axis=concat_dim, tiled=True)
    blocks = jnp.split(filled, [sum(widths[:k]) for k in range(1, len(widths))], axis=along)
    return tuple(
        (b.reshape(*filled.shape[:along], *a.shape[along:]) for a, b in zip(arrays, blocks))
    )


def in_order(blocks, dim):
    dims = list(blocks.shape[1:])
    dims[dim] *= blocks.shape[0]
    return jnp.moveaxis(blocks, 0, dim).reshape(dims)


def gather_directly(value, axis, dim):
    return in_order(copy_for_each(value, axis), dim)


def shards(features, key_grads, error_in, selected, bin_edges, threshold, moment, second, master):
    highest = lax.Precision.HIGHEST
    whole = lax.all_gather(features, "tensor", axis=0, tiled=True)
    summed = lax.dot_general(
        whole, key_grads, (((0,), (0,)), ((), ())), preferred_element_type=jnp.float32
    )
    summed = summed + error_in[0].astype(jnp.float32)
    row_total = summed.shape[0]
    width_head = summed.shape[1]
    owners = lax.axis_size("dp")
    region = row_total // owners
    squares = jnp.sum(summed * summed, axis=1)
    row_ids = lax.iota(jnp.int32, row_total)
    member = (
        (row_ids[:, None] >= bin_edges[None, :-1]) & (row_ids[:, None] < bin_edges[None, 1:])
    ).astype(jnp.float32)
    energy = over_copies(jnp.dot(squares, member, precision=highest), "dp")
    widths = (bin_edges[1:] - bin_edges[:-1]).astype(jnp.float32)
    levels = lax.iota(jnp.int32, widths.shape[0])
    normal = 1.0 / jnp.sqrt(energy / (owners * width_head * widths) + epsilon)
    scale = jnp.where(levels >= threshold[0], normal, jnp.ones_like(normal))
    row_scale = jnp.dot(member, scale, precision=highest)
    chosen_ids = selected[0, 0]
    chosen = jnp.zeros((row_total,), jnp.float32).at[chosen_ids].set(1.0)
    kept = summed * chosen[:, None]
    error_out = (summed - kept).astype(jnp.bfloat16)[None]
    scaled = kept * row_scale[:, None]
    owner_of = chosen_ids // region
    owner_hot = (owner_of[:, None] == lax.iota(jnp.int32, owners)[None, :]).astype(jnp.int32)
    earlier = jnp.cumsum(owner_hot, axis=0) - owner_hot
    rank = jnp.sum(earlier * owner_hot, axis=1)
    slot = owner_of * CAP + rank
    outgoing = jnp.zeros((owners * CAP, width_head), jnp.float32).at[slot].set(scaled[chosen_ids])
    offsets = (
        jnp.full((owners * CAP,), region, jnp.float32)
        .at[slot]
        .set((chosen_ids % region).astype(jnp.float32))
    )
    arrived, places = in_one_piece(
        (outgoing.reshape(owners, CAP, width_head), offsets.reshape(owners, CAP)), "dp", 0, 0, 2
    )
    place_hot = (places.reshape(-1)[:, None] == lax.iota(jnp.float32, region)[None, :]).astype(
        jnp.float32
    )
    grad = lax.dot_general(
        place_hot, arrived.reshape(-1, width_head), (((0,), (0,)), ((), ())), precision=highest
    )
    moment_new = beta_first * moment + (1.0 - beta_first) * grad
    second_new = beta_second * second + (1.0 - beta_second) * grad * grad
    first_hat = moment_new / (1.0 - beta_first**step_count)
    second_hat = second_new / (1.0 - beta_second**step_count)
    master_new = master - learn_rate * (
        first_hat / (jnp.sqrt(second_hat) + adam_epsilon) + decay_rate * master
    )
    weight = master_new.astype(jnp.bfloat16)
    keys = jnp.dot(whole, gather_directly(weight, "dp", 0), preferred_element_type=jnp.float32)
    return (keys.astype(jnp.bfloat16), error_out, moment_new, second_new, master_new)


def solution(mesh):
    in_specs = (
        P(("dp", "tensor"), None),
        P("dp", "tensor"),
        P("dp", None, "tensor"),
        P("dp", "tensor", None),
        P(),
        P(),
        P("dp", "tensor"),
        P("dp", "tensor"),
        P("dp", "tensor"),
    )
    out_specs = (
        P("dp", "tensor"),
        P("dp", None, "tensor"),
        P("dp", "tensor"),
        P("dp", "tensor"),
        P("dp", "tensor"),
    )
    return jax.shard_map(shards, mesh=mesh, in_specs=in_specs, out_specs=out_specs, check_vma=False)
```

profile of v0, /device:TPU:1, one launch (start us, length us, event | category | flops | bytes accessed | tf_op | source)
XLA Modules:
  0.0 216.0 jit_solution(11072930889191832977)
XLA Ops:
  7.2 0.0 copy-start
  7.2 0.0 copy-start.5
  7.2 0.0 copy-start.4
  7.2 0.0 all-gather.2.cloned.1.call-start
  7.2 0.7 all-gather.2.cloned.1.call-update
  7.9 1.5 copy.28
  9.4 0.0 copy-done.5
  9.5 0.1 fusion.15
  9.5 0.2 reduce_window_sum.11
  9.7 0.2 select_reduce_fusion
  9.9 0.0 copy-done.4
  9.9 0.1 fusion.41
  10.0 103.0 %all-gather.2.cloned.1.call-done = bf16[1024,4096]{1,0:T(8,128)(2,1)} async-done(((bf16[128,4096]{1,0:T(8,128)(2,1)}), bf16[1024,4096]{1,0:T(8,128)(2,1)}) %all-gather.2.cloned.1.call-update) | async-done | bytes 8388624 | tf_op jit(solution)/shard_map/all_gather | solution.py:53
  112.9 0.0 copy-done
  112.9 4.9 %multiply_reduce_fusion = (f32[4096]{0:T(1024)S(1)}, f32[4096,128]{0,1:T(8,128)S(1)}) fusion(bf16[1,4096,128]{1,2,0:T(8,128)(2,1)S(1)} %copy.28, bf16[1024,4096]{1,0:T(8,128)(2,1)} %all-gather.2.cloned.1.call-done, bf16[1024,128]{1,0:T(8,128)(2,1)S(1)} %copy-done), kind=kOutput, calls=%fused_computation.8 | convolution fusion | flops 1075834880 | bytes 11812864 | tf_op jit(solution)/shard_map/dot_general | solution.py:54
  117.8 0.3 convolution_bitcast_fusion
  118.2 0.7 broadcast_in_dim.17
  118.8 10.5 %all-to-all-start = ((f32[64,1,16]{2,1,0:T(1,128)}), f32[64,1,16]{2,1,0:T(1,128)S(1)}, u32[]{:S(2)}, u32[]{:S(2)}) async-start(f32[64,1,16]{2,1,0:T(1,128)} %broadcast_in_dim.17), calls=%async_computation | async-start | bytes 65536 | tf_op jit(solution)/shard_map/all_to_all | solution.py:19
  130.1 1.0 scatter_custom_fusion.2
  131.0 0.9 reshape_reshape.4
  132.0 1.0 scatter_custom_fusion
  133.0 5.7 %all-to-all-done = f32[64,1,16]{2,1,0:T(1,128)S(1)} async-done(((f32[64,1,16]{2,1,0:T(1,128)}), f32[64,1,16]{2,1,0:T(1,128)S(1)}, u32[]{:S(2)}, u32[]{:S(2)}) %all-to-all-start) | async-done | bytes 4128 | tf_op jit(solution)/shard_map/all_to_all | solution.py:19
  138.6 0.1 reduce_sum.32
  138.7 0.3 fusion.4
  139.0 1.7 fusion.2
  140.8 1.9 copy.30
  142.7 1.9 scatter_custom_fusion.1
  144.6 1.0 reshape.153
  145.5 1.0 pad_maximum_fusion
  146.5 0.0 copy-start.1
  146.5 0.0 copy-start.2
  146.6 0.0 copy-start.3
  146.6 0.5 reshape.204
  147.0 15.6 %all_to_all.16 = f32[64,1,774]{2,1,0:T(1,128)S(1)} all-to-all(f32[64,1,774]{2,1,0:T(1,128)S(1)} %reshape.204), channel_id=1, replica_groups=mesh['dp'=64,'tensor'=8] {'dp'}, dimensions={0} | all-to-all | bytes 396288 | tf_op jit(solution)/shard_map/all_to_all | solution.py:34
  162.6 0.5 broadcast.187
  163.1 1.2 reduce.3
  164.3 0.3 reshape.205
  164.6 0.1 slice_reduce_fusion
  164.8 0.1 eq.33
  164.9 0.0 copy-done.1
  164.9 0.0 copy-done.2
  164.9 0.0 copy-done.3
  164.9 1.1 fusion.39
  166.0 1.3 broadcast_in_dim.19
  167.3 6.2 %all-to-all-start.2 = ((bf16[64,64,128]{2,1,0:T(8,128)(2,1)}), bf16[64,64,128]{2,1,0:T(8,128)(2,1)S(1)}, u32[]{:S(2)}, u32[]{:S(2)}) async-start(bf16[64,64,128]{2,1,0:T(8,128)(2,1)} %broadcast_in_dim.19), calls=%async_computation.2 | async-start | bytes 2097152 | tf_op jit(solution)/shard_map/all_to_all | solution.py:19
  173.5 1.3 copy.33
  174.8 27.2 %all-to-all-done.2 = bf16[64,64,128]{2,1,0:T(8,128)(2,1)S(1)} async-done(((bf16[64,64,128]{2,1,0:T(8,128)(2,1)}), bf16[64,64,128]{2,1,0:T(8,128)(2,1)S(1)}, u32[]{:S(2)}, u32[]{:S(2)}) %all-to-all-start.2) | async-done | bytes 1048608 | tf_op jit(solution)/shard_map/all_to_all | solution.py:19
  202.0 6.3 %fusion.1 = bf16[1024,128]{0,1:T(8,128)(2,1)S(1)} fusion(bf16[4096,128]{1,0:T(8,128)(2,1)S(1)} %bitcast.57, bf16[1024,4096]{1,0:T(8,128)(2,1)} %all-gather.2.cloned.1.call-done), kind=kOutput, calls=%fused_computation.10 | convolution fusion | flops 1073872896 | bytes 9699328 | tf_op jit(solution)/shard_map/dot_general | solution.py:106
  208.3 0.8 copy.32
  (6 shorter events, 0.1 us)
Async XLA Ops:
  7.2 105.8 %copy-start = (bf16[1024,128]{1,0:T(8,128)(2,1)S(1)}, bf16[1024,128]{1,0:T(8,128)(2,1)}, u32[]{:S(2)}) copy-start(bf16[1024,128]{1,0:T(8,128)(2,1)} %param.10) | copy-start | bytes 786436
  7.2 2.2 %copy-start.5 = (s32[1,1,128]{2,1,0:T(1,128)S(1)}, s32[1,1,128]{2,1,0:T(1,128)}, u32[]{:S(2)}) copy-start(s32[1,1,128]{2,1,0:T(1,128)} %param.12) | copy-start | bytes 1540
  7.2 2.7 %copy-start.4 = (s32[17]{0:T(128)S(1)}, s32[17]{0:T(128)}, u32[]{:S(2)}) copy-start(s32[17]{0:T(128)} %param.13) | copy-start | bytes 208
  7.2 105.7 %all-gather.2.cloned.1.call-start = ((), (), s32[]{:S(2)}) async-start(), calls=%async_computation.3 | async-start | bytes 9437184 | tf_op jit(solution)/shard_map/all_gather | solution.py:53
  118.8 19.8 %all-to-all-start = ((f32[64,1,16]{2,1,0:T(1,128)}), f32[64,1,16]{2,1,0:T(1,128)S(1)}, u32[]{:S(2)}, u32[]{:S(2)}) async-start(f32[64,1,16]{2,1,0:T(1,128)} %broadcast_in_dim.17), calls=%async_computation | async-start | bytes 65536 | tf_op jit(solution)/shard_map/all_to_all | solution.py:19
  146.5 18.4 %copy-start.1 = (f32[64,128]{1,0:T(8,128)S(1)}, f32[64,128]{1,0:T(8,128)}, u32[]{:S(2)}) copy-start(f32[64,128]{1,0:T(8,128)} %param.17) | copy-start | bytes 98308
  146.5 18.4 %copy-start.2 = (f32[64,128]{1,0:T(8,128)S(1)}, f32[64,128]{1,0:T(8,128)}, u32[]{:S(2)}) copy-start(f32[64,128]{1,0:T(8,128)} %param.15) | copy-start | bytes 98308
  146.6 18.4 %copy-start.3 = (f32[64,128]{1,0:T(8,128)S(1)}, f32[64,128]{1,0:T(8,128)}, u32[]{:S(2)}) copy-start(f32[64,128]{1,0:T(8,128)} %param.16) | copy-start | bytes 98308
  167.3 34.7 %all-to-all-start.2 = ((bf16[64,64,128]{2,1,0:T(8,128)(2,1)}), bf16[64,64,128]{2,1,0:T(8,128)(2,1)S(1)}, u32[]{:S(2)}, u32[]{:S(2)}) async-start(bf16[64,64,128]{2,1,0:T(8,128)(2,1)} %broadcast_in_dim.19), calls=%async_computation.2 | async-start | bytes 2097152 | tf_op jit(solution)/shard_map/all_to_all | solution.py:19
Sparse Core Ops, SparseCore 0:
  10.1 102.8 all-gather.1
where the time goes:
time: 217 us; the launch traced here: 216 us
  waiting for transfers between devices  137 us (63%)
  starting transfers between devices  16.8 us (8%)
  blocking collectives  15.6 us (7%)
  local copies, waits for them, and re-layouts  14.9 us (7%)
  between operations  14.9 us (7%)
  matrix products  12.8 us (6%)
  other arithmetic  4.47 us (2%)
    all_gather x1, waiting for transfers between devices, shards(): whole = lax.all_gather(features, 'tensor', axis=0, tiled=True)  103 us
    all_to_all x2, waiting for transfers between devices, copy_for_each(): lax.all_to_all(jnp.broadcast_to(value[None], (devices, *value.shape)), ax...  32.9 us
    all_to_all x2, starting transfers between devices, copy_for_each(): lax.all_to_all(jnp.broadcast_to(value[None], (devices, *value.shape)), ax...  16.7 us
    all_to_all x1, blocking collectives, in_one_piece(): lax.all_to_all(both, axis, split_axis=split_dim, concat_axis=concat_dim,...  15.6 us
    dot_general x1, matrix products, shards(): jnp.dot(whole, gather_directly(weight, 'dp', 0), preferred_element_type=j...  6.29 us
    dot_general x1, matrix products, shards(): lax.dot_general(whole, key_grads, (((0,), (0,)), ((), ())), preferred_ele...  4.88 us
    unnamed x17, local copies, waits for them, and re-layouts  4.38 us
  transfers between devices with their start and end apart: 3, of which 3 were waited for; matrix products, arithmetic and copies ran while one was open for 3% of the time, Pallas kernels for 0%

commit v1 on v0

--- a/solution.py
+++ b/solution.py
@@ -12,6 +12,12 @@
 epsilon = 1e-06
 adam_epsilon = 1e-08
 step_count = 10.0
+
+
+def gather_by_exchange(x, axis, dim):
+    size = lax.axis_size(axis)
+    repeats = [size if d == dim else 1 for d in range(x.ndim)]
+    return lax.all_to_all(jnp.tile(x, repeats), axis, split_axis=dim, concat_axis=dim, tiled=True)
 
 
 def copy_for_each(value, axis):
@@ -50,7 +56,7 @@
 
 def shards(features, key_grads, error_in, selected, bin_edges, threshold, moment, second, master):
     highest = lax.Precision.HIGHEST
-    whole = lax.all_gather(features, "tensor", axis=0, tiled=True)
+    whole = gather_by_exchange(features, "tensor", 0)
     summed = lax.dot_general(
         whole, key_grads, (((0,), (0,)), ((), ())), preferred_element_type=jnp.float32
     )

time: 217 us -> 301 us (1.39)
  waiting for transfers between devices: 137 us -> 219 us
  between operations: 14.9 us -> 1.52 us
  starting transfers between devices: 16.8 us -> 27.8 us
  local copies, waits for them, and re-layouts: 14.9 us -> 19.6 us
    all_to_all x0 -> x1, waiting for transfers between devices: none -> 186 us  [gather_by_exchange(): lax.all_to_all(jnp.tile(x, repeats), axis, split_axis=dim, concat_axis=di...]
    all_gather x1 -> x0, waiting for transfers between devices: 103 us -> none  [shards(): whole = lax.all_gather(features, 'tensor', axis=0, tiled=True)]
    all_to_all x0 -> x1, starting transfers between devices: none -> 11 us  [gather_by_exchange(): lax.all_to_all(jnp.tile(x, repeats), axis, split_axis=dim, concat_axis=di...]
    another operation x0 -> x1, local copies, waits for them, and re-layouts: none -> 5.53 us  [gather_by_exchange(): jnp.tile(x, repeats)]
  transfers between devices with their start and end apart: 3 -> 3, of which waited for: 3 -> 3; matrix products, arithmetic and copies ran while one was open for 3% -> 2% of each run, Pallas kernels for 0% -> 0%
where the time goes in v1:
time: 301 us; the launch traced here: 300 us
  waiting for transfers between devices  219 us (73%)
  starting transfers between devices  27.8 us (9%)
  local copies, waits for them, and re-layouts  19.6 us (7%)
  blocking collectives  15.6 us (5%)
  matrix products  12.8 us (4%)
  other arithmetic  4.47 us (1%)
    all_to_all x1, waiting for transfers between devices, gather_by_exchange(): lax.all_to_all(jnp.tile(x, repeats), axis, split_axis=dim, concat_axis=di...  186 us
    all_to_all x2, waiting for transfers between devices, copy_for_each(): lax.all_to_all(jnp.broadcast_to(value[None], (devices, *value.shape)), ax...  32.9 us
    all_to_all x2, starting transfers between devices, copy_for_each(): lax.all_to_all(jnp.broadcast_to(value[None], (devices, *value.shape)), ax...  16.8 us
    all_to_all x1, blocking collectives, in_one_piece(): lax.all_to_all(both, axis, split_axis=split_dim, concat_axis=concat_dim,...  15.6 us
    all_to_all x1, starting transfers between devices, gather_by_exchange(): lax.all_to_all(jnp.tile(x, repeats), axis, split_axis=dim, concat_axis=di...  11 us
    dot_general x1, matrix products, shards(): jnp.dot(whole, gather_directly(weight, 'dp', 0), preferred_element_type=j...  6.28 us
  transfers between devices with their start and end apart: 3, of which 3 were waited for; matrix products, arithmetic and copies ran while one was open for 2% of the time, Pallas kernels for 0%

profile of v1, /device:TPU:1, one launch (start us, length us, event | category | flops | bytes accessed | tf_op | source)
XLA Modules:
  0.0 300.3 jit_solution(16659596157775822518)
XLA Ops:
  0.6 0.0 copy-start
  0.6 5.5 %tile.2 = bf16[8,128,4096]{2,1,0:T(8,128)(2,1)} broadcast(bf16[128,4096]{1,0:T(8,128)(2,1)} %param.9), dimensions={1,2} | broadcast | bytes 9437184 | tf_op jit(solution)/shard_map/tile | solution.py:20
  6.2 0.0 copy-start.1
  6.2 11.0 %all-to-all-start = ((bf16[8,128,4096]{2,1,0:T(8,128)(2,1)}), bf16[8,128,4096]{2,1,0:T(8,128)(2,1)}, u32[]{:S(2)}, u32[]{:S(2)}) async-start(bf16[8,128,4096]{2,1,0:T(8,128)(2,1)} %tile.2), calls=%async_computation | async-start | bytes 16777216 | tf_op jit(solution)/shard_map/all_to_all | solution.py:20
  17.2 0.0 copy-done.1
  17.2 0.0 copy-start.6
  17.2 0.0 copy-start.5
  17.2 0.5 copy.28
  17.7 0.1 copy-done.6
  17.8 0.1 fusion.15
  17.9 0.2 reduce_window_sum.11
  18.1 0.2 select_reduce_fusion
  18.3 0.0 copy-done.5
  18.3 0.1 fusion.41
  18.4 185.7 %all-to-all-done = bf16[8,128,4096]{2,1,0:T(8,128)(2,1)} async-done(((bf16[8,128,4096]{2,1,0:T(8,128)(2,1)}), bf16[8,128,4096]{2,1,0:T(8,128)(2,1)}, u32[]{:S(2)}, u32[]{:S(2)}) %all-to-all-start) | async-done | bytes 8388640 | tf_op jit(solution)/shard_map/all_to_all | solution.py:20
  204.0 0.0 copy-done
  204.1 4.9 %multiply_reduce_fusion = (f32[4096]{0:T(1024)S(1)}, f32[4096,128]{0,1:T(8,128)S(1)}) fusion(bf16[1,4096,128]{1,2,0:T(8,128)(2,1)S(1)} %copy.28, bf16[1024,4096]{1,0:T(8,128)(2,1)} %bitcast.4, bf16[1024,128]{1,0:T(8,128)(2,1)S(1)} %copy-done), kind=kOutput, calls=%fused_computation.8 | convolution fusion | flops 1075834880 | bytes 11812864 | tf_op jit(solution)/shard_map/dot_general | solution.py:60
  208.9 0.3 convolution_bitcast_fusion
  209.3 0.7 broadcast_in_dim.17
  209.9 10.6 %all-to-all-start.1 = ((f32[64,1,16]{2,1,0:T(1,128)}), f32[64,1,16]{2,1,0:T(1,128)S(1)}, u32[]{:S(2)}, u32[]{:S(2)}) async-start(f32[64,1,16]{2,1,0:T(1,128)} %broadcast_in_dim.17), calls=%async_computation.1 | async-start | bytes 65536 | tf_op jit(solution)/shard_map/all_to_all | solution.py:25
  221.2 1.0 scatter_custom_fusion.2
  222.2 0.9 reshape_reshape.4
  223.1 1.0 scatter_custom_fusion
  224.1 5.7 %all-to-all-done.1 = f32[64,1,16]{2,1,0:T(1,128)S(1)} async-done(((f32[64,1,16]{2,1,0:T(1,128)}), f32[64,1,16]{2,1,0:T(1,128)S(1)}, u32[]{:S(2)}, u32[]{:S(2)}) %all-to-all-start.1) | async-done | bytes 4128 | tf_op jit(solution)/shard_map/all_to_all | solution.py:25
  229.8 0.1 reduce_sum.32
  229.9 0.3 fusion.4
  230.2 1.7 fusion.2
  231.9 1.9 copy.30
  233.8 1.9 scatter_custom_fusion.1
  235.7 1.0 reshape.160
  236.7 1.0 pad_maximum_fusion
  237.7 0.0 copy-start.2
  237.7 0.0 copy-start.3
  237.7 0.0 copy-start.4
  237.7 0.5 reshape.211
  238.2 15.6 %all_to_all.25 = f32[64,1,774]{2,1,0:T(1,128)S(1)} all-to-all(f32[64,1,774]{2,1,0:T(1,128)S(1)} %reshape.211), channel_id=1, replica_groups=mesh['dp'=64,'tensor'=8] {'dp'}, dimensions={0} | all-to-all | bytes 396288 | tf_op jit(solution)/shard_map/all_to_all | solution.py:40
  253.8 0.5 broadcast.190
  254.3 1.2 reduce.3
  255.5 0.3 reshape.212
  255.7 0.1 slice_reduce_fusion
  255.9 0.1 eq.33
  256.1 0.0 copy-done.2
  256.1 0.0 copy-done.3
  256.1 0.0 copy-done.4
  256.1 1.1 fusion.39
  257.1 1.3 broadcast_in_dim.19
  258.5 6.2 %all-to-all-start.3 = ((bf16[64,64,128]{2,1,0:T(8,128)(2,1)}), bf16[64,64,128]{2,1,0:T(8,128)(2,1)S(1)}, u32[]{:S(2)}, u32[]{:S(2)}) async-start(bf16[64,64,128]{2,1,0:T(8,128)(2,1)} %broadcast_in_dim.19), calls=%async_computation.3 | async-start | bytes 2097152 | tf_op jit(solution)/shard_map/all_to_all | solution.py:25
  264.7 1.3 copy.33
  266.0 27.2 %all-to-all-done.3 = bf16[64,64,128]{2,1,0:T(8,128)(2,1)S(1)} async-done(((bf16[64,64,128]{2,1,0:T(8,128)(2,1)}), bf16[64,64,128]{2,1,0:T(8,128)(2,1)S(1)}, u32[]{:S(2)}, u32[]{:S(2)}) %all-to-all-start.3) | async-done | bytes 1048608 | tf_op jit(solution)/shard_map/all_to_all | solution.py:25
  293.2 6.3 %fusion.1 = bf16[1024,128]{0,1:T(8,128)(2,1)S(1)} fusion(bf16[4096,128]{1,0:T(8,128)(2,1)S(1)} %bitcast.58, bf16[1024,4096]{1,0:T(8,128)(2,1)} %bitcast.4), kind=kOutput, calls=%fused_computation.10 | convolution fusion | flops 1073872896 | bytes 9699328 | tf_op jit(solution)/shard_map/dot_general | solution.py:112
  299.5 0.8 copy.32
  (6 shorter events, 0.1 us)
Async XLA Ops:
  0.6 203.4 %copy-start = (bf16[1024,128]{1,0:T(8,128)(2,1)S(1)}, bf16[1024,128]{1,0:T(8,128)(2,1)}, u32[]{:S(2)}) copy-start(bf16[1024,128]{1,0:T(8,128)(2,1)} %param.10) | copy-start | bytes 786436
  6.2 11.0 %copy-start.1 = (bf16[1,4096,128]{2,1,0:T(8,128)(2,1)S(1)}, bf16[1,4096,128]{2,1,0:T(8,128)(2,1)}, u32[]{:S(2)}) copy-start(bf16[1,4096,128]{2,1,0:T(8,128)(2,1)} %param.11) | copy-start | bytes 3145732
  6.2 197.9 %all-to-all-start = ((bf16[8,128,4096]{2,1,0:T(8,128)(2,1)}), bf16[8,128,4096]{2,1,0:T(8,128)(2,1)}, u32[]{:S(2)}, u32[]{:S(2)}) async-start(bf16[8,128,4096]{2,1,0:T(8,128)(2,1)} %tile.2), calls=%async_computation | async-start | bytes 16777216 | tf_op jit(solution)/shard_map/all_to_all | solution.py:20
  17.2 0.7 copy-start.6
  17.2 1.1 copy-start.5
  209.9 19.9 %all-to-all-start.1 = ((f32[64,1,16]{2,1,0:T(1,128)}), f32[64,1,16]{2,1,0:T(1,128)S(1)}, u32[]{:S(2)}, u32[]{:S(2)}) async-start(f32[64,1,16]{2,1,0:T(1,128)} %broadcast_in_dim.17), calls=%async_computation.1 | async-start | bytes 65536 | tf_op jit(solution)/shard_map/all_to_all | solution.py:25
  237.7 18.4 %copy-start.2 = (f32[64,128]{1,0:T(8,128)S(1)}, f32[64,128]{1,0:T(8,128)}, u32[]{:S(2)}) copy-start(f32[64,128]{1,0:T(8,128)} %param.17) | copy-start | bytes 98308
  237.7 18.4 %copy-start.3 = (f32[64,128]{1,0:T(8,128)S(1)}, f32[64,128]{1,0:T(8,128)}, u32[]{:S(2)}) copy-start(f32[64,128]{1,0:T(8,128)} %param.15) | copy-start | bytes 98308
  237.7 18.4 %copy-start.4 = (f32[64,128]{1,0:T(8,128)S(1)}, f32[64,128]{1,0:T(8,128)}, u32[]{:S(2)}) copy-start(f32[64,128]{1,0:T(8,128)} %param.16) | copy-start | bytes 98308
  258.5 34.7 %all-to-all-start.3 = ((bf16[64,64,128]{2,1,0:T(8,128)(2,1)}), bf16[64,64,128]{2,1,0:T(8,128)(2,1)S(1)}, u32[]{:S(2)}, u32[]{:S(2)}) async-start(bf16[64,64,128]{2,1,0:T(8,128)(2,1)} %broadcast_in_dim.19), calls=%async_computation.3 | async-start | bytes 2097152 | tf_op jit(solution)/shard_map/all_to_all | solution.py:25
